TPU v7x, 256 devices: a whole 4x4x8 slice. The times are simulated.
256 devices in a mesh: tm: 8 (over z_hi, x), chan: 32 (over z_lo, y, core).
Axes of the slice: x: 4, y: 4, z: 8 (z_hi: 2, z_lo: 4; z = z_hi * 4 + z_lo), core: 2. Of those that a mesh axis runs over, the one named last changes fastest.
Arguments:
- voltage_frequency_samples: bfloat16 [2, 256, 30, 2, 8192], P(None, ('tm', 'chan')), may hold values from -6 to 6
- lag_lookup_entry: int32 [8, 8, 30], P('tm'), may hold values from 0 to 63
- lag_lookup_turning: float32 [64, 8192], P(None, 'chan'), may hold values from -3.140625 to 3.140625
- antenna_pair_members: int32 [435, 2], replicated, may hold values from 0 to 29, as said below
- frequency_bin_target: int32 [8192], P('chan'), may hold values from 0 to 63, as said below
Outputs:
- centre_vis: float32 [512, 2, 4, 435], P(('tm', 'chan'))
Inputs may be any that keep to these rules, and one draw needn't show every extreme that they name: `antenna_pair_members`: every unordered pair of two different stations of the 30 appears in exactly one row, in either order. `frequency_bin_target`: each of the 64 output channels receives exactly 128 fine channels.
All inputs are finite; a program needn't handle non-finite values.
Results may differ from a plain program's by a relative error of at most 0.0029.
Values may be sent and summed in bfloat16 or wider, within the bound.
A program may use at most 128 MiB of HBM per device.

v0:
```python
import jax
import jax.numpy as jnp
from jax import lax
from jax.sharding import PartitionSpec as P

F = 8192
Q = 64
G_DEV = 1


def correlate(left_part, right_part):
    return jnp.einsum("gtaf,gtbf->gabf", left_part, right_part, preferred_element_type=jnp.float32)


def on_device(
    voltage_frequency_samples,
    lag_lookup_entry,
    lag_lookup_turning,
    antenna_pair_members,
    frequency_bin_target,
):
    regrouped = lax.all_to_all(
        voltage_frequency_samples, "chan", split_axis=4, concat_axis=1, tiled=True
    )
    fine_local = regrouped.shape[4]
    selector = (frequency_bin_target[:, None] == jnp.arange(Q, dtype=jnp.int32)[None, :]).astype(
        jnp.bfloat16
    )
    spectra_count = regrouped.shape[1]
    stations = regrouped.shape[2]
    polars = regrouped.shape[3]
    antenna_pair_total = antenna_pair_members.shape[0]
    shaped = regrouped.reshape(2, G_DEV, spectra_count // G_DEV, stations * polars, fine_local)
    real_part = shaped[0]
    imag_part = shaped[1]
    vis_real = correlate(real_part, real_part) + correlate(imag_part, imag_part)
    vis_imag = correlate(imag_part, real_part) - correlate(real_part, imag_part)
    left_antenna_number = antenna_pair_members[:, 0]
    right_antenna_number = antenna_pair_members[:, 1]
    full_shape = (G_DEV, stations, polars, stations, polars, fine_local)
    picked_real = vis_real.reshape(full_shape)[:, left_antenna_number, :, right_antenna_number]
    picked_imag = vis_imag.reshape(full_shape)[:, left_antenna_number, :, right_antenna_number]
    base_real = jnp.transpose(picked_real, (1, 2, 3, 0, 4)).reshape(
        G_DEV, polars * polars, antenna_pair_total, fine_local
    )
    base_imag = jnp.transpose(picked_imag, (1, 2, 3, 0, 4)).reshape(
        G_DEV, polars * polars, antenna_pair_total, fine_local
    )
    station_phase = jnp.take(lag_lookup_turning, lag_lookup_entry, axis=0)
    phase_diff = (
        station_phase[:, :, left_antenna_number] - station_phase[:, :, right_antenna_number]
    )
    cosine = jnp.cos(phase_diff)
    sine = jnp.sin(phase_diff)
    centres = lag_lookup_entry.shape[1]
    partial_list = []
    for centre in range(centres):
        cos_now = cosine[:, centre][:, None]
        sin_now = sine[:, centre][:, None]
        rot_real = (base_real * cos_now + base_imag * sin_now).astype(jnp.bfloat16)
        rot_imag = (base_imag * cos_now - base_real * sin_now).astype(jnp.bfloat16)
        rotated = jnp.stack([rot_real, rot_imag])
        partial_list.append(
            jnp.einsum("rgpbf,fq->qrpb", rotated, selector, preferred_element_type=jnp.float32)
        )
    partial_value = jnp.stack(partial_list)
    columns = selector.shape[1]
    tail = (2, polars * polars, antenna_pair_total)
    flat = partial_value.reshape((centres * columns,) + tail)
    channel_summed_products = lax.psum_scatter(
        flat, ("tm", "chan"), scatter_dimension=0, tiled=True
    )
    return channel_summed_products * (Q / F)


def solution(mesh):
    return jax.shard_map(
        on_device,
        mesh=mesh,
        in_specs=(
            P(None, ("tm", "chan"), None, None, None),
            P("tm", None, None),
            P(None, "chan"),
            P(),
            P("chan"),
        ),
        out_specs=P(("tm", "chan"), None, None, None),
        check_vma=False,
    )
```

profile of v0, /device:TPU:97, one launch (start us, length us, event | category | flops | bytes accessed | tf_op | source)
XLA Modules:
  0.0 534.2 jit_solution(12457336647658863745)
XLA Ops:
  6.5 19.7 %copy.43 = bf16[2,1,30,2,8192]{2,3,1,0,4:T(2,128)(2,1)} copy(bf16[2,1,30,2,8192]{4,3,2,1,0:T(2,128)(2,1)} %param.5) | data formatting | bytes 3932160 | tf_op args[0]
  26.2 17.3 %reshape.729 = bf16[32,2,15360]{2,1,0:T(2,128)(2,1)} reshape(bf16[8192,2,1,2,30]{4,3,2,1,0:T(2,128)(2,1)} %bitcast.325) | data formatting | bytes 3932160
  43.5 8.3 %all-to-all-start = ((bf16[32,2,15360]{2,1,0:T(2,128)(2,1)}), bf16[32,2,15360]{2,1,0:T(2,128)(2,1)S(1)}, u32[]{:S(2)}, u32[]{:S(2)}) async-start(bf16[32,2,15360]{2,1,0:T(2,128)(2,1)} %reshape.729), calls=%async_computation | async-start | bytes 3932160 | tf_op jit(solution)/shard_map/all_to_all | solution.py:22
  56.5 2.9 gather_fusion.3
  59.4 13.8 %cosine_bitcast_fusion = (f32[1,8,435,256]{3,1,2,0:T(8,128)S(1)}, f32[1,8,435,256]{3,1,2,0:T(8,128)S(1)}) fusion(f32[435,8,256]{2,1,0:T(8,128)} %gather_fusion.2, f32[435,8,256]{2,1,0:T(8,128)} %gather_fusion.3), kind=kLoop, calls=%fused_computation.8 | loop fusion | flops 890880 | bytes 14254080 | tf_op jit(solution)/shard_map/cos | solution.py:53
  91.1 4.9 all-to-all-done
  95.9 24.0 %reshape.730 = bf16[8192,2,1,2,30]{4,3,2,1,0:T(2,128)(2,1)} reshape(bf16[32,2,15360]{2,1,0:T(2,128)(2,1)S(1)} %all-to-all-done) | data formatting | bytes 3932160
  119.9 12.3 %copy.62 = bf16[2,1,30,2,32,256]{5,4,3,2,1,0:T(8,128)(2,1)S(1)} copy(bf16[2,1,30,2,32,256]{2,3,0,5,4,1:T(2,128)(2,1)} %bitcast.324) | data formatting | bytes 3932160 | tf_op jit(solution)/shard_map/all_to_all | solution.py:22
  133.4 5.3 copy.45
  138.7 4.2 copy.47
  142.9 6.9 %fusion.101 = f32[256,60,60]{2,1,0:T(8,128)} fusion(bf16[32,60,256]{1,0,2:T(8,128)(2,1)} %copy.45), kind=kOutput, calls=%fused_computation.169 | convolution fusion | flops 58982400 | bytes 4669440 | tf_op jit(solution)/shard_map/gtaf,gtbf->gabf/dot_general | solution.py:12
  151.2 4.6 subtract_bitcast_fusion
  155.7 8.6 %copy.57 = f32[1,60,60,256]{3,2,1,0:T(8,128)} copy(f32[1,60,60,256]{1,2,3,0:T(8,128)} %subtract_bitcast_fusion) | data formatting | bytes 7372800 | tf_op jit(solution)/shard_map/sub | solution.py:37
  164.3 5.6 %reshape.712 = f32[30,2,30,2,256]{4,3,2,1,0:T(2,128)} reshape(f32[1,60,60,256]{3,2,1,0:T(8,128)} %copy.57) | data formatting | bytes 7372800 | tf_op jit(solution)/shard_map/reshape | solution.py:42
  169.9 8.1 %gather_fusion.4 = f32[435,2,2,256]{3,2,1,0:T(2,128)} fusion(f32[30,2,30,2,256]{4,3,2,1,0:T(2,128)} %reshape.712, s32[435]{0:T(512)S(1)} %bitcast.322), kind=kCustom, calls=%fused_computation.4 | custom fusion | bytes 3567000 | tf_op jit(solution)/shard_map/gather | solution.py:42
  178.0 3.1 copy.58
  181.1 7.9 %add_bitcast_fusion = f32[1,60,60,256]{1,2,3,0:T(8,128)} fusion(f32[256,60,60]{2,1,0:T(8,128)} %fusion.101, bf16[32,60,256]{1,0,2:T(8,128)(2,1)S(1)} %copy.47), kind=kOutput, calls=%fused_computation.6 | convolution fusion | flops 59904000 | bytes 8355840 | tf_op jit(solution)/shard_map/gtaf,gtbf->gabf/dot_general | solution.py:12
  189.1 8.6 %copy.49 = f32[1,60,60,256]{3,2,1,0:T(8,128)} copy(f32[1,60,60,256]{1,2,3,0:T(8,128)} %add_bitcast_fusion) | data formatting | bytes 7372800 | tf_op jit(solution)/shard_map/add | solution.py:36
  197.7 5.6 %reshape.676 = f32[30,2,30,2,256]{4,3,2,1,0:T(2,128)} reshape(f32[1,60,60,256]{3,2,1,0:T(8,128)} %copy.49) | data formatting | bytes 7372800 | tf_op jit(solution)/shard_map/reshape | solution.py:41
  203.4 7.0 %gather_fusion = f32[435,2,2,256]{3,2,1,0:T(2,128)S(1)} fusion(f32[30,2,30,2,256]{4,3,2,1,0:T(2,128)} %reshape.676, s32[435]{0:T(512)S(1)} %bitcast.323), kind=kCustom, calls=%fused_computation | custom fusion | bytes 3567000 | tf_op jit(solution)/shard_map/gather | solution.py:41
  212.3 7.7 %fusion.53 = (bf16[1,1,4,435,256]{4,3,2,0,1:T(8,128)(2,1)S(1)}, bf16[1,1,4,435,256]{4,3,2,0,1:T(8,128)(2,1)S(1)}, bf16[1,1,4,435,256]{4,3,2,0,1:T(8,128)(2,1)S(1...) fusion(f32[1,2,2,435,256]{4,3,2,1,0:T(8,128)S(1)} %copy-done.3,, ...), kind=kLoop, calls=%fused_computation.86 | loop fusion | flops 28508160 | bytes 24944640 | tf_op jit(solution)/shard_map/convert_element_type | solution.py:60
  226.7 4.3 copy.59
  231.0 12.0 %copy.60 = f32[512,2,4,435]{3,2,1,0:T(4,128)} copy(f32[512,2,4,435]{3,0,2,1:T(8,128)} %bitcast.326) | data formatting | bytes 14254080 | tf_op jit(solution)/shard_map/reshape | solution.py:69
  243.0 282.7 %all-reduce.3.cloned.1.call-done = f32[512,2,4,435]{3,2,1,0:T(4,128)} async-done(((f32[512,2,4,435]{3,2,1,0:T(4,128)}), f32[512,2,4,435]{3,2,1,0:T(4,128)}) %all-reduce.3.cloned.1.call-update) | async-done | bytes 7127056
  (73 shorter events, 34.9 us)
Async XLA Ops:
  6.5 45.8 %copy-start = (f32[64,256]{1,0:T(8,128)S(1)}, f32[64,256]{1,0:T(8,128)}, u32[]{:S(2)}) copy-start(f32[64,256]{1,0:T(8,128)} %param.7) | copy-start | bytes 196612
  43.5 8.7 %copy-start.12 = (s32[1,8,30]{2,1,0:T(8,128)S(1)}, s32[1,8,30]{2,1,0:T(8,128)}, u32[]{:S(2)}) copy-start(s32[1,8,30]{2,1,0:T(8,128)} %param.6) | copy-start | bytes 2884
  43.5 52.4 %all-to-all-start = ((bf16[32,2,15360]{2,1,0:T(2,128)(2,1)}), bf16[32,2,15360]{2,1,0:T(2,128)(2,1)S(1)}, u32[]{:S(2)}, u32[]{:S(2)}) async-start(bf16[32,2,15360]{2,1,0:T(2,128)(2,1)} %reshape.729), calls=%async_computation | async-start | bytes 3932160 | tf_op jit(solution)/shard_map/all_to_all | solution.py:22
  51.9 1.6 copy-start.13
  51.9 473.8 %all-reduce.3.cloned.1.call-start = ((), (), s32[]{:S(2)}) async-start(), calls=%async_computation.1 | async-start | bytes 16777216
  142.9 6.9 %copy-start.2 = (bf16[32,60,256]{1,0,2:T(8,128)(2,1)S(1)}, bf16[32,60,256]{1,0,2:T(8,128)(2,1)}, u32[]{:S(2)}) copy-start(bf16[32,60,256]{1,0,2:T(8,128)(2,1)} %copy.45) | copy-start | bytes 2949124
  203.3 7.4 %copy-start.8 = (f32[1,1,435,256]{3,2,1,0:T(8,128)S(1)}, f32[1,1,435,256]{3,2,1,0:T(8,128)}, u32[]{:S(2)}) copy-start(f32[1,1,435,256]{3,2,1,0:T(8,128)} %copy.102) | copy-start | bytes 1336324
  203.3 7.4 %copy-start.9 = (f32[1,1,435,256]{3,2,1,0:T(8,128)S(1)}, f32[1,1,435,256]{3,2,1,0:T(8,128)}, u32[]{:S(2)}) copy-start(f32[1,1,435,256]{3,2,1,0:T(8,128)} %copy.103) | copy-start | bytes 1336324
  203.3 7.4 %copy-start.10 = (f32[1,1,435,256]{3,2,1,0:T(8,128)S(1)}, f32[1,1,435,256]{3,2,1,0:T(8,128)}, u32[]{:S(2)}) copy-start(f32[1,1,435,256]{3,2,1,0:T(8,128)} %copy.104) | copy-start | bytes 1336324
  210.4 1.5 copy-start.3
  210.4 1.5 copy-start.4
  210.4 1.7 copy-start.5
  210.4 1.8 copy-start.6
  210.4 1.9 copy-start.7
  212.3 7.7 %copy-start.14 = (s32[256]{0:T(256)S(1)}, s32[256]{0:T(256)}, u32[]{:S(2)}) copy-start(s32[256]{0:T(256)} %param.9) | copy-start | bytes 3076
  220.0 2.2 copy-start.11
  243.0 284.1 %copy-start.1 = (f32[64,256]{1,0:T(8,128)S(1)}, f32[64,256]{1,0:T(8,128)}, u32[]{:S(2)}) copy-start(f32[64,256]{1,0:T(8,128)} %param.7) | copy-start | bytes 196612
Sparse Core Ops, SparseCore 0:
  243.1 282.5 all-reduce.2
where the time goes:
time: 539 us; the launch traced here: 534 us
  waiting for transfers between devices  288 us (53%)
  local copies, waits for them, and re-layouts  173 us (32%)
  matrix products  27.4 us (5%)
  other arithmetic  23.1 us (4%)
  between operations  14 us (3%)
  starting transfers between devices  8.68 us (2%)
    unnamed x2, waiting for transfers between devices  283 us
    unnamed x49, local copies, waits for them, and re-layouts  75.5 us
    dot_general x4, matrix products, correlate(): jnp.einsum('gtaf,gtbf->gabf', left_part, right_part, preferred_element_ty...  20.8 us
    cos x1, other arithmetic, on_device(): cosine = jnp.cos(phase_diff)  13.8 us
    all_to_all x1, local copies, waits for them, and re-layouts, on_device(): lax.all_to_all(voltage_frequency_samples, 'chan', split_axis=4, concat_ax...  12.3 us
    reshape x1, local copies, waits for them, and re-layouts, on_device(): flat = partial_value.reshape((centres * columns,) + tail)  12 us
  transfers between devices with their start and end apart: 2, of which 2 were waited for; matrix products, arithmetic and copies ran while one was open for 7% of the time, Pallas kernels for 0%

commit v1 on v0

--- a/solution.py
+++ b/solution.py
@@ -19,8 +19,14 @@
     antenna_pair_members,
     frequency_bin_target,
 ):
-    regrouped = lax.all_to_all(
-        voltage_frequency_samples, "chan", split_axis=4, concat_axis=1, tiled=True
+    regrouped = jnp.concatenate(
+        lax.all_to_all(
+            jnp.stack(jnp.split(voltage_frequency_samples, lax.axis_size("chan"), axis=4)),
+            axis_name="chan",
+            split_axis=0,
+            concat_axis=0,
+        ),
+        axis=1,
     )
     fine_local = regrouped.shape[4]
     selector = (frequency_bin_target[:, None] == jnp.arange(Q, dtype=jnp.int32)[None, :]).astype(

time: 539 us -> 514 us (0.954)
  local copies, waits for them, and re-layouts: 173 us -> 149 us
    unnamed x49 -> x79, local copies, waits for them, and re-layouts: 75.5 us -> 60.9 us
    all_to_all x1 -> x0, local copies, waits for them, and re-layouts: 12.3 us -> none  [on_device(): lax.all_to_all(voltage_frequency_samples, 'chan', split_axis=4, concat_ax...]
  transfers between devices with their start and end apart: 2 -> 2, of which waited for: 2 -> 2; matrix products, arithmetic and copies ran while one was open for 7% -> 8% of each run, Pallas kernels for 0% -> 0%
where the time goes in v1:
time: 514 us; the launch traced here: 509 us
  waiting for transfers between devices  288 us (56%)
  local copies, waits for them, and re-layouts  149 us (29%)
  matrix products  27.5 us (5%)
  other arithmetic  23.1 us (4%)
  between operations  14 us (3%)
  starting transfers between devices  8.68 us (2%)
    unnamed x2, waiting for transfers between devices  283 us
    unnamed x79, local copies, waits for them, and re-layouts  60.9 us
    dot_general x4, matrix products, correlate(): jnp.einsum('gtaf,gtbf->gabf', left_part, right_part, preferred_element_ty...  20.8 us
    cos x1, other arithmetic, on_device(): cosine = jnp.cos(phase_diff)  13.8 us
    reshape x1, local copies, waits for them, and re-layouts, on_device(): flat = partial_value.reshape((centres * columns,) + tail)  12 us
  transfers between devices with their start and end apart: 2, of which 2 were waited for; matrix products, arithmetic and copies ran while one was open for 8% of the time, Pallas kernels for 0%

profile of v1, /device:TPU:97, one launch (start us, length us, event | category | flops | bytes accessed | tf_op | source)
XLA Modules:
  0.0 509.4 jit_solution(3702456891122394076)
XLA Ops:
  54.4 8.3 %all-to-all-start = ((bf16[32,2,1,30,2,256]{5,4,3,1,2,0:T(2,128)(2,1)}), bf16[32,2,1,30,2,256]{5,4,3,1,2,0:T(2,128)(2,1)S(1)}, u32[]{:S(2)}, u32[]{:S(2)}) async-start(bf16[32,2,1,30,2,256]{5,4,3,1,2,0:T(2,128)(2,1)} %constant_dynamic-update-slice_fusion), calls=%async_computation | async-start | bytes 3932160 | tf_op jit(solution)/shard_map/all_to_all | solution.py:23
  64.5 2.9 gather_fusion.2
  67.4 2.9 gather_fusion.3
  70.3 13.8 %cosine_bitcast_fusion = (f32[1,8,435,256]{3,1,2,0:T(8,128)S(1)}, f32[1,8,435,256]{3,1,2,0:T(8,128)S(1)}) fusion(f32[435,8,256]{2,1,0:T(8,128)} %gather_fusion.2, f32[435,8,256]{2,1,0:T(8,128)} %gather_fusion.3), kind=kLoop, calls=%fused_computation.8 | loop fusion | flops 890880 | bytes 14254080 | tf_op jit(solution)/shard_map/cos | solution.py:59
  84.2 2.4 fusion.99
  87.4 2.4 fusion.98
  102.0 4.8 all-to-all-done
  109.1 4.4 copy.108
  113.7 4.2 copy.111
  117.9 6.9 %fusion.101 = f32[256,60,60]{2,1,0:T(8,128)} fusion(bf16[32,60,256]{1,0,2:T(8,128)(2,1)} %copy.108), kind=kOutput, calls=%fused_computation.201 | convolution fusion | flops 58982400 | bytes 4669440 | tf_op jit(solution)/shard_map/gtaf,gtbf->gabf/dot_general | solution.py:12
  126.2 4.6 subtract_bitcast_fusion
  130.8 8.6 %copy.121 = f32[1,60,60,256]{3,2,1,0:T(8,128)} copy(f32[1,60,60,256]{1,2,3,0:T(8,128)} %subtract_bitcast_fusion) | data formatting | bytes 7372800 | tf_op jit(solution)/shard_map/sub | solution.py:43
  139.4 5.6 %reshape.714 = f32[30,2,30,2,256]{4,3,2,1,0:T(2,128)} reshape(f32[1,60,60,256]{3,2,1,0:T(8,128)} %copy.121) | data formatting | bytes 7372800 | tf_op jit(solution)/shard_map/reshape | solution.py:48
  145.0 8.1 %gather_fusion.4 = f32[435,2,2,256]{3,2,1,0:T(2,128)} fusion(f32[30,2,30,2,256]{4,3,2,1,0:T(2,128)} %reshape.714, s32[435]{0:T(512)S(1)} %bitcast.383), kind=kCustom, calls=%fused_computation.4 | custom fusion | bytes 3567000 | tf_op jit(solution)/shard_map/gather | solution.py:48
  153.1 3.1 copy.122
  156.2 8.0 %add_bitcast_fusion = f32[1,60,60,256]{1,2,3,0:T(8,128)} fusion(f32[256,60,60]{2,1,0:T(8,128)} %fusion.101, bf16[32,60,256]{1,0,2:T(8,128)(2,1)S(1)} %copy.111), kind=kOutput, calls=%fused_computation.6 | convolution fusion | flops 59904000 | bytes 8355840 | tf_op jit(solution)/shard_map/gtaf,gtbf->gabf/dot_general | solution.py:12
  164.2 8.6 %copy.113 = f32[1,60,60,256]{3,2,1,0:T(8,128)} copy(f32[1,60,60,256]{1,2,3,0:T(8,128)} %add_bitcast_fusion) | data formatting | bytes 7372800 | tf_op jit(solution)/shard_map/add | solution.py:42
  172.8 5.6 %reshape.678 = f32[30,2,30,2,256]{4,3,2,1,0:T(2,128)} reshape(f32[1,60,60,256]{3,2,1,0:T(8,128)} %copy.113) | data formatting | bytes 7372800 | tf_op jit(solution)/shard_map/reshape | solution.py:47
  178.5 7.0 %gather_fusion = f32[435,2,2,256]{3,2,1,0:T(2,128)S(1)} fusion(f32[30,2,30,2,256]{4,3,2,1,0:T(2,128)} %reshape.678, s32[435]{0:T(512)S(1)} %bitcast.384), kind=kCustom, calls=%fused_computation | custom fusion | bytes 3567000 | tf_op jit(solution)/shard_map/gather | solution.py:47
  187.5 7.7 %fusion.53 = (bf16[1,1,4,435,256]{4,3,2,0,1:T(8,128)(2,1)S(1)}, bf16[1,1,4,435,256]{4,3,2,0,1:T(8,128)(2,1)S(1)}, bf16[1,1,4,435,256]{4,3,2,0,1:T(8,128)(2,1)S(1...) fusion(f32[1,2,2,435,256]{4,3,2,1,0:T(8,128)S(1)} %copy-done.3,, ...), kind=kLoop, calls=%fused_computation.86 | loop fusion | flops 28508160 | bytes 24944640 | tf_op jit(solution)/shard_map/convert_element_type | solution.py:66
  195.2 2.2 fusion.71
  201.8 4.3 copy.123
  206.1 12.0 %copy.124 = f32[512,2,4,435]{3,2,1,0:T(4,128)} copy(f32[512,2,4,435]{3,0,2,1:T(8,128)} %bitcast.385) | data formatting | bytes 14254080 | tf_op jit(solution)/shard_map/reshape | solution.py:75
  218.2 282.7 %all-reduce.3.cloned.1.call-done = f32[512,2,4,435]{3,2,1,0:T(4,128)} async-done(((f32[512,2,4,435]{3,2,1,0:T(4,128)}), f32[512,2,4,435]{3,2,1,0:T(4,128)}) %all-reduce.3.cloned.1.call-update) | async-done | bytes 7127056
  (105 shorter events, 74.1 us)
Async XLA Ops:
  6.5 56.7 %copy-start = (f32[64,256]{1,0:T(8,128)S(1)}, f32[64,256]{1,0:T(8,128)}, u32[]{:S(2)}) copy-start(f32[64,256]{1,0:T(8,128)} %param.7) | copy-start | bytes 196612
  54.4 8.7 %copy-start.13 = (s32[1,8,30]{2,1,0:T(8,128)S(1)}, s32[1,8,30]{2,1,0:T(8,128)}, u32[]{:S(2)}) copy-start(s32[1,8,30]{2,1,0:T(8,128)} %param.6) | copy-start | bytes 2884
  54.4 52.4 %all-to-all-start = ((bf16[32,2,1,30,2,256]{5,4,3,1,2,0:T(2,128)(2,1)}), bf16[32,2,1,30,2,256]{5,4,3,1,2,0:T(2,128)(2,1)S(1)}, u32[]{:S(2)}, u32[]{:S(2)}) async-start(bf16[32,2,1,30,2,256]{5,4,3,1,2,0:T(2,128)(2,1)} %constant_dynamic-update-slice_fusion), calls=%async_computation | async-start | bytes 3932160 | tf_op jit(solution)/shard_map/all_to_all | solution.py:23
  62.7 1.6 copy-start.14
  62.7 438.1 %all-reduce.3.cloned.1.call-start = ((), (), s32[]{:S(2)}) async-start(), calls=%async_computation.1 | async-start | bytes 16777216
  109.1 4.4 copy-start.4
  117.9 7.0 %copy-start.2 = (bf16[32,60,256]{1,0,2:T(8,128)(2,1)S(1)}, bf16[32,60,256]{1,0,2:T(8,128)(2,1)}, u32[]{:S(2)}) copy-start(bf16[32,60,256]{1,0,2:T(8,128)(2,1)} %copy.108) | copy-start | bytes 2949124
  178.5 7.4 %copy-start.9 = (f32[1,1,435,256]{3,2,1,0:T(8,128)S(1)}, f32[1,1,435,256]{3,2,1,0:T(8,128)}, u32[]{:S(2)}) copy-start(f32[1,1,435,256]{3,2,1,0:T(8,128)} %copy.165) | copy-start | bytes 1336324
  178.5 7.4 %copy-start.10 = (f32[1,1,435,256]{3,2,1,0:T(8,128)S(1)}, f32[1,1,435,256]{3,2,1,0:T(8,128)}, u32[]{:S(2)}) copy-start(f32[1,1,435,256]{3,2,1,0:T(8,128)} %copy.166) | copy-start | bytes 1336324
  178.5 7.4 %copy-start.11 = (f32[1,1,435,256]{3,2,1,0:T(8,128)S(1)}, f32[1,1,435,256]{3,2,1,0:T(8,128)}, u32[]{:S(2)}) copy-start(f32[1,1,435,256]{3,2,1,0:T(8,128)} %copy.167) | copy-start | bytes 1336324
  185.5 1.5 copy-start.3
  185.5 1.5 copy-start.5
  185.5 1.7 copy-start.6
  185.5 1.8 copy-start.7
  185.5 1.9 copy-start.8
  187.5 7.7 %copy-start.15 = (s32[256]{0:T(256)S(1)}, s32[256]{0:T(256)}, u32[]{:S(2)}) copy-start(s32[256]{0:T(256)} %param.9) | copy-start | bytes 3076
  195.1 2.2 copy-start.12
  218.2 284.1 %copy-start.1 = (f32[64,256]{1,0:T(8,128)S(1)}, f32[64,256]{1,0:T(8,128)}, u32[]{:S(2)}) copy-start(f32[64,256]{1,0:T(8,128)} %param.7) | copy-start | bytes 196612
Sparse Core Ops, SparseCore 0:
  218.3 282.5 all-reduce.2
